TPU v7x, 32 devices: a whole 2x2x4 slice. The times are simulated.
32 devices in a mesh: groups: 2 (over x), blk: 4 (over y, core), width: 4 (over z).
Axes of the slice: x: 2, y: 2, z: 4, core: 2. Of those that a mesh axis runs over, the one named last changes fastest.
Arguments:
- activations: float32 [8192, 8192], P(('groups', 'blk'), 'width'), parts along dimension 0, may hold values from -6 to 6
- query_grads: float32 [16, 8192, 128], P(('groups', 'blk'), 'width'), parts along dimension 0, may hold values from -0.0625 to 0.0625
- outgrad_proj: float32 [8192, 128], P(('groups', 'blk', 'width')), parts along dimension 0, may hold values from -0.6 to 0.6
- doc_ids: int32 [8192], P(('groups', 'blk', 'width')), parts along dimension 0, may hold values from 0 to 15, never falling along the last dimension, each value on 1 to 512 neighbouring positions
Outputs:
- token_scores: float32 [8192, 8], P(('groups', 'blk', 'width')), parts along dimension 0
- doc_scores: float32 [32, 8], P('groups'), parts along dimension 0
There are 2 independent parts, one for each index of `groups`. A program takes and returns all parts, laid end to end along the dimension named above; each array names one. Nothing has to cross between parts.
Inputs may be any that keep to these rules, and one draw needn't show every extreme that they name: `doc_ids`: never falls along the tokens; every document 0 to 15 holds 1 to 512 tokens, one exactly 512.
All inputs are finite; a program needn't handle non-finite values.
Results may differ from a plain program's by a relative error of at most 0.000078.
Values sent between devices are 32-bit elements; how exact they have to be, the bound alone decides.
No kernel may reach another device: no remote copies, remote signals or barrier semaphores. Data moves between devices by JAX's collectives and lax.ppermute only.
A program may use at most 128 MiB of HBM per device.

v0:
```python
import jax
import jax.numpy as jnp
from jax import lax
from jax.sharding import PartitionSpec as P

DOC_BLK = 4


def per_device(activations, query_grads, outgrad_proj, doc_ids):
    projected = jnp.einsum(
        "td,qdr->tqr",
        activations,
        lax.all_gather(query_grads, "blk", axis=0, tiled=True),
        precision=lax.Precision.HIGHEST,
        preferred_element_type=jnp.float32,
    )
    owned_parts = lax.psum_scatter(projected, "width", scatter_dimension=0, tiled=True)
    token_scores = jnp.sum(owned_parts * outgrad_proj[:, None, :], axis=2)
    doc_total = DOC_BLK * lax.axis_size("blk")
    doc_range = jnp.arange(doc_total, dtype=jnp.int32)
    onehot = (doc_ids[:, None] == doc_range[None, :]).astype(jnp.float32)
    doc_sums = jnp.einsum(
        "tn,tq->nq",
        onehot,
        token_scores,
        precision=lax.Precision.HIGHEST,
        preferred_element_type=jnp.float32,
    )
    doc_counts = jnp.sum(onehot, axis=0)
    doc_sums, doc_counts = lax.psum((doc_sums, doc_counts), ("blk", "width"))
    doc_scores = doc_sums / jnp.sqrt(doc_counts)[:, None]
    return (token_scores, doc_scores)


def solution(mesh):
    return jax.shard_map(
        per_device,
        mesh=mesh,
        in_specs=(
            P(("groups", "blk"), "width"),
            P(("groups", "blk"), "width", None),
            P(("groups", "blk", "width"), None),
            P(("groups", "blk", "width")),
        ),
        out_specs=(P(("groups", "blk", "width"), None), P("groups", None)),
        check_vma=False,
    )
```

profile of v0, /device:TPU:0, one launch (start us, length us, event | category | flops | bytes accessed | tf_op | source)
XLA Modules:
  0.0 222.9 jit_solution(11770008080408502427)
XLA Ops:
  7.2 0.0 all-gather.2.cloned.1.call-start
  7.2 0.7 all-gather.2.cloned.1.call-update
  7.9 0.0 copy-start.2
  7.9 0.0 copy-start
  7.9 0.0 reduce-scatter.2.cloned.1.call-start
  8.0 62.6 %all-gather.2.cloned.1.call-done = f32[8,2048,128]{2,1,0:T(8,128)} async-done(((f32[2,2048,128]{2,1,0:T(8,128)}), f32[8,2048,128]{2,1,0:T(8,128)}) %all-gather.2.cloned.1.call-update) | async-done | bytes 8388624 | tf_op jit(solution)/shard_map/all_gather | solution.py:13
  70.6 32.7 %fusion = f32[1024,8,128]{2,0,1:T(8,128)} fusion(f32[8,2048,128]{2,1,0:T(8,128)} %all-gather.2.cloned.1.call-done, f32[1024,2048]{1,0:T(8,128)} %param.4), kind=kOutput, calls=%fused_computation | convolution fusion | flops 25769803776 | bytes 20971520 | tf_op jit(solution)/shard_map/td,qdr->tqr/dot_general | solution.py:10
  103.3 0.0 reduce-scatter.2.cloned.1.call-update
  103.3 0.0 copy-done.2
  103.3 0.1 convert_reduce_fusion
  103.4 76.8 %reduce-scatter.2.cloned.1.call-done = f32[256,8,128]{2,0,1:T(8,128)} async-done(((f32[1024,8,128]{2,0,1:T(8,128)}), f32[256,8,128]{2,0,1:T(8,128)}) %reduce-scatter.2.cloned.1.call-update) | async-done | bytes 1048592 | tf_op jit(solution)/shard_map/reduce_scatter | solution.py:17
  180.2 0.0 copy-done
  180.2 1.6 multiply_reduce_fusion
  181.8 0.0 copy-start.1
  181.8 0.1 fusion.2
  181.9 33.5 %all-reduce = (f32[16,8]{0,1:T(8,128)S(1)}, f32[16]{0:T(128)S(1)}) all-reduce(f32[16,8]{0,1:T(8,128)S(1)} %fusion.2, f32[16]{0:T(128)S(1)} %convert_reduce_fusion), channel_id=1, replica_groups=mesh['groups'=2,'blk'=4,'width'=4] {'blk','width'}, use_global_device_ids=true, to_apply=%region_2.0 | all-reduce | flops 144 | bytes 1152 | tf_op jit(solution)/shard_map/psum | solution.py:30
  215.5 0.6 broadcast_divide_fusion
  216.1 0.0 copy-done.1
  (1 shorter events, 0.0 us)
Async XLA Ops:
  7.2 63.4 %all-gather.2.cloned.1.call-start = ((), (), s32[]{:S(2)}) async-start(), calls=%async_computation.1 | async-start | bytes 10485760 | tf_op jit(solution)/shard_map/all_gather | solution.py:13
  7.9 95.4 %copy-start.2 = (s32[256]{0:T(256)S(1)}, s32[256]{0:T(256)}, u32[]{:S(2)}) copy-start(s32[256]{0:T(256)} %param.7) | copy-start | bytes 3076
  7.9 172.3 %copy-start = (f32[256,128]{1,0:T(8,128)S(1)}, f32[256,128]{1,0:T(8,128)}, u32[]{:S(2)}) copy-start(f32[256,128]{1,0:T(8,128)} %param.6) | copy-start | bytes 393220
  7.9 172.3 %reduce-scatter.2.cloned.1.call-start = ((), (), s32[]{:S(2)}) async-start(), calls=%async_computation.2 | async-start | bytes 5242880 | tf_op jit(solution)/shard_map/reduce_scatter | solution.py:17
  181.8 34.3 %copy-start.1 = (f32[256,8]{0,1:T(8,128)}, f32[256,8]{0,1:T(8,128)S(1)}, u32[]{:S(2)}) copy-start(f32[256,8]{0,1:T(8,128)S(1)} %multiply_reduce_fusion) | copy-start | bytes 24580
Sparse Core Ops, SparseCore 0:
  9.6 60.9 all-gather.1
  103.4 76.7 reduce-scatter.1
where the time goes:
time: 223 us
  waiting for transfers between devices  140 us (63%)
  blocking collectives  33.5 us (15%)
  matrix products  32.8 us (15%)
  between operations  14.1 us (6%)
  other arithmetic  2.29 us (1%)
    reduce_scatter x1, waiting for transfers between devices, per_device(): lax.psum_scatter(projected, 'width', scatter_dimension=0, tiled=True)  76.8 us
    all_gather x1, waiting for transfers between devices, per_device(): lax.all_gather(query_grads, 'blk', axis=0, tiled=True)  62.6 us
    psum x1, blocking collectives, per_device(): doc_sums, doc_counts = lax.psum((doc_sums, doc_counts), ('blk', 'width'))  33.5 us
    dot_general x1, matrix products, per_device(): jnp.einsum('td,qdr->tqr', activations, lax.all_gather(query_grads, 'blk',...  32.7 us
  transfers between devices with their start and end apart: 2, of which 2 were waited for; matrix products, arithmetic and copies ran while one was open for 0% of the time, Pallas kernels for 0%

commit v1 on v0

--- a/solution.py
+++ b/solution.py
@@ -27,7 +27,7 @@
         preferred_element_type=jnp.float32,
     )
     doc_counts = jnp.sum(onehot, axis=0)
-    doc_sums, doc_counts = lax.psum((doc_sums, doc_counts), ("blk", "width"))
+    doc_sums, doc_counts = lax.psum(lax.psum((doc_sums, doc_counts), "width"), "blk")
     doc_scores = doc_sums / jnp.sqrt(doc_counts)[:, None]
     return (token_scores, doc_scores)
 

time: 223 us -> 206 us (0.924)
  blocking collectives: 33.5 us -> 16.8 us
    psum x1 -> x2, blocking collectives: 33.5 us -> 16.8 us  [the longest x1 11.1 us: per_device(): lax.psum((doc_sums, doc_counts), 'width')]
where the time goes in v1:
time: 206 us
  waiting for transfers between devices  140 us (68%)
  matrix products  32.8 us (16%)
  blocking collectives  16.8 us (8%)
  between operations  14.1 us (7%)
  other arithmetic  2.29 us (1%)
    reduce_scatter x1, waiting for transfers between devices, per_device(): lax.psum_scatter(projected, 'width', scatter_dimension=0, tiled=True)  76.8 us
    all_gather x1, waiting for transfers between devices, per_device(): lax.all_gather(query_grads, 'blk', axis=0, tiled=True)  62.6 us
    dot_general x1, matrix products, per_device(): jnp.einsum('td,qdr->tqr', activations, lax.all_gather(query_grads, 'blk',...  32.7 us
    psum x1, blocking collectives, per_device(): lax.psum((doc_sums, doc_counts), 'width')  11.1 us
    psum x1, blocking collectives, per_device(): lax.psum(lax.psum((doc_sums, doc_counts), 'width'), 'blk')  5.76 us
  transfers between devices with their start and end apart: 2, of which 2 were waited for; matrix products, arithmetic and copies ran while one was open for 0% of the time, Pallas kernels for 0%

profile of v1, /device:TPU:0, one launch (start us, length us, event | category | flops | bytes accessed | tf_op | source)
XLA Modules:
  0.0 206.2 jit_solution(6521173511257590659)
XLA Ops:
  7.2 0.0 all-gather.2.cloned.1.call-start
  7.2 0.7 all-gather.2.cloned.1.call-update
  7.9 0.0 copy-start.2
  7.9 0.0 copy-start
  7.9 0.0 reduce-scatter.2.cloned.1.call-start
  8.0 62.6 %all-gather.2.cloned.1.call-done = f32[8,2048,128]{2,1,0:T(8,128)} async-done(((f32[2,2048,128]{2,1,0:T(8,128)}), f32[8,2048,128]{2,1,0:T(8,128)}) %all-gather.2.cloned.1.call-update) | async-done | bytes 8388624 | tf_op jit(solution)/shard_map/all_gather | solution.py:13
  70.6 32.7 %fusion = f32[1024,8,128]{2,0,1:T(8,128)} fusion(f32[8,2048,128]{2,1,0:T(8,128)} %all-gather.2.cloned.1.call-done, f32[1024,2048]{1,0:T(8,128)} %param.4), kind=kOutput, calls=%fused_computation | convolution fusion | flops 25769803776 | bytes 20971520 | tf_op jit(solution)/shard_map/td,qdr->tqr/dot_general | solution.py:10
  103.3 0.0 reduce-scatter.2.cloned.1.call-update
  103.3 0.0 copy-done.2
  103.3 0.1 convert_reduce_fusion
  103.4 76.8 %reduce-scatter.2.cloned.1.call-done = f32[256,8,128]{2,0,1:T(8,128)} async-done(((f32[1024,8,128]{2,0,1:T(8,128)}), f32[256,8,128]{2,0,1:T(8,128)}) %reduce-scatter.2.cloned.1.call-update) | async-done | bytes 1048592 | tf_op jit(solution)/shard_map/reduce_scatter | solution.py:17
  180.2 0.0 copy-done
  180.2 1.6 multiply_reduce_fusion
  181.8 0.0 copy-start.1
  181.8 0.1 fusion.2
  181.9 11.1 %all-reduce = (f32[16,8]{0,1:T(8,128)S(1)}, f32[16]{0:T(128)S(1)}) all-reduce(f32[16,8]{0,1:T(8,128)S(1)} %fusion.2, f32[16]{0:T(128)S(1)} %convert_reduce_fusion), channel_id=1, replica_groups=mesh['groups'=2,'blk'=4,'width'=4] {'width'}, use_global_device_ids=true, to_apply=%region_2.0 | all-reduce | flops 144 | bytes 1152 | tf_op jit(solution)/shard_map/psum | solution.py:30
  193.0 5.8 %all-reduce.1 = (f32[16,8]{0,1:T(8,128)S(1)}, f32[16]{0:T(128)S(1)}) all-reduce(f32[16,8]{0,1:T(8,128)S(1)} %get-tuple-element.2, f32[16]{0:T(128)S(1)} %get-tuple-element.3), channel_id=1, replica_groups=mesh['groups'=2,'blk'=4,'width'=4] {'blk'}, use_global_device_ids=true, to_apply=%region_3.0 | all-reduce | flops 144 | bytes 1152 | tf_op jit(solution)/shard_map/psum | solution.py:30
  198.8 0.6 broadcast_divide_fusion
  199.4 0.0 copy-done.1
  (1 shorter events, 0.0 us)
Async XLA Ops:
  7.2 63.4 %all-gather.2.cloned.1.call-start = ((), (), s32[]{:S(2)}) async-start(), calls=%async_computation.1 | async-start | bytes 10485760 | tf_op jit(solution)/shard_map/all_gather | solution.py:13
  7.9 95.4 %copy-start.2 = (s32[256]{0:T(256)S(1)}, s32[256]{0:T(256)}, u32[]{:S(2)}) copy-start(s32[256]{0:T(256)} %param.7) | copy-start | bytes 3076
  7.9 172.3 %copy-start = (f32[256,128]{1,0:T(8,128)S(1)}, f32[256,128]{1,0:T(8,128)}, u32[]{:S(2)}) copy-start(f32[256,128]{1,0:T(8,128)} %param.6) | copy-start | bytes 393220
  7.9 172.3 %reduce-scatter.2.cloned.1.call-start = ((), (), s32[]{:S(2)}) async-start(), calls=%async_computation.2 | async-start | bytes 5242880 | tf_op jit(solution)/shard_map/reduce_scatter | solution.py:17
  181.8 17.6 %copy-start.1 = (f32[256,8]{0,1:T(8,128)}, f32[256,8]{0,1:T(8,128)S(1)}, u32[]{:S(2)}) copy-start(f32[256,8]{0,1:T(8,128)S(1)} %multiply_reduce_fusion) | copy-start | bytes 24580
Sparse Core Ops, SparseCore 0:
  9.6 60.9 all-gather.1
  103.4 76.7 reduce-scatter.1
